TPU v7x, 256 devices: a whole 4x4x8 slice. The times are simulated.
256 devices in a mesh: dp: 16 (over y_hi, x, core), expert: 16 (over y_lo, z).
Axes of the slice: x: 4, y: 4 (y_hi: 2, y_lo: 2; y = y_hi * 2 + y_lo), z: 8, core: 2. Of those that a mesh axis runs over, the one named last changes fastest.
Arguments:
- tokens: bfloat16 [32768, 3072], P(('dp', 'expert')), parts along dimension 0, may hold values from -6 to 6
- w_gate: bfloat16 [3072, 8192], P(None, 'expert'), may hold values from -0.109375 to 0.109375
- w_up: bfloat16 [3072, 8192], P(None, 'expert'), may hold values from -0.109375 to 0.109375
- w_down: bfloat16 [8192, 3072], P('expert'), may hold values from -0.0625 to 0.0625
- route_ids: int32 [32768, 2], P(('dp', 'expert')), parts along dimension 0, may hold values from 0 to 7, as said below
- route_prob: float32 [32768], P(('dp', 'expert')), parts along dimension 0, may hold values from 0.5 to 0.95
- slot_index: int32 [32768], P(('dp', 'expert')), parts along dimension 0, may hold values from 0 to 64, as said below
Outputs:
- mixed: bfloat16 [32768, 3072], P(('dp', 'expert')), parts along dimension 0
There are 16 independent parts, one for each index of `dp`. A program takes and returns all parts, laid end to end along the dimension named above; an argument that names none is the same for every part. Nothing has to cross between parts.
Inputs may be any that keep to these rules, and one draw needn't show every extreme that they name: `route_ids`: each row names two different experts. `slot_index`: a token of whose two experts one is expert 0 holds its rank, in row order, among the tokens of its device that name expert 0; every other token holds 64. At most 64 of one device's 128 tokens name expert 0, and some device has exactly 64; the router's capacity of 64 tokens for expert 0 is counted over each aligned pair of 256 tokens (blocks 2k and 2k + 1) and is always filled, so those two devices have exactly 64 such tokens together.
All inputs are finite; a program needn't handle non-finite values.
Results may differ from a plain program's by a relative error of at most 0.023.
Values may be sent and summed in bfloat16 or wider, within the bound.
No kernel may reach another device: no remote copies, remote signals or barrier semaphores. Data moves between devices by JAX's collectives and lax.ppermute only.
A program may use at most 128 MiB of HBM per device.

v0:
```python
import jax
import jax.numpy as jnp
from jax import lax
from jax.sharding import PartitionSpec as P


def shards(tokens, w_gate, w_up, w_down, route_ids, route_prob, slot_index):
    local_count = tokens.shape[0]
    capacity = local_count // 2
    share = jnp.where(
        route_ids[:, 0] == 0, route_prob, jnp.where(route_ids[:, 1] == 0, 1.0 - route_prob, 0.0)
    )
    share = jnp.where(slot_index < capacity, share, 0.0)
    picker = slot_index[None, :] == jnp.arange(capacity, dtype=jnp.int32)[:, None]
    picker_half = picker.astype(jnp.bfloat16)
    source = jnp.dot(picker_half, tokens, preferred_element_type=jnp.float32).astype(jnp.bfloat16)
    row_share = jnp.dot(picker.astype(jnp.float32), share, precision=lax.Precision.HIGHEST)
    block = lax.all_gather(source, "expert", axis=0, tiled=True)
    gate = jnp.dot(block, w_gate, preferred_element_type=jnp.float32)
    up = jnp.dot(block, w_up, preferred_element_type=jnp.float32)
    hidden = (jax.nn.silu(gate) * up).astype(jnp.bfloat16)
    partial_value = jnp.dot(hidden, w_down, preferred_element_type=jnp.float32).astype(jnp.bfloat16)
    partial_value = lax.optimization_barrier(partial_value)
    terms = partial_value.astype(jnp.float32)
    down = lax.psum_scatter(
        terms.astype(jnp.bfloat16), "expert", scatter_dimension=0, tiled=True
    ).astype(jnp.float32)
    scaled = (row_share[:, None] * down).astype(jnp.bfloat16)
    placed = jnp.einsum("cr,cd->rd", picker_half, scaled, preferred_element_type=jnp.float32)
    return placed.astype(jnp.bfloat16)


def solution(mesh):
    return jax.shard_map(
        shards,
        mesh=mesh,
        in_specs=(
            P(("dp", "expert"), None),
            P(None, "expert"),
            P(None, "expert"),
            P("expert", None),
            P(("dp", "expert"), None),
            P(("dp", "expert")),
            P(("dp", "expert")),
        ),
        out_specs=P(("dp", "expert"), None),
        check_vma=False,
    )
```

profile of v0, /device:TPU:4, one launch (start us, length us, event | category | flops | bytes accessed | tf_op | source)
XLA Modules:
  0.0 208.1 jit_solution(16924911761300009242)
XLA Ops:
  6.5 0.0 copy-start
  6.5 0.0 all-gather.2.cloned.1.call-start
  6.5 2.3 %convolution_convert_fusion.2 = bf16[64,3072]{1,0:T(8,128)(2,1)} fusion(bf16[128,3072]{1,0:T(8,128)(2,1)} %param.7, s32[128]{0:T(128)} %param.13), kind=kOutput, calls=%fused_computation.2 | convolution fusion | flops 50536448 | bytes 1180160 | tf_op jit(solution)/shard_map/dot_general | solution.py:16
  8.8 0.0 all-gather.2.cloned.1.call-update
  8.9 0.0 reduce-scatter.2.cloned.1.call-start
  8.9 85.4 %all-gather.2.cloned.1.call-done = bf16[1024,3072]{1,0:T(8,128)(2,1)} async-done(((bf16[64,3072]{1,0:T(8,128)(2,1)}), bf16[1024,3072]{1,0:T(8,128)(2,1)}) %all-gather.2.cloned.1.call-update) | async-done | bytes 6291472 | tf_op jit(solution)/shard_map/all_gather | solution.py:18
  94.3 8.5 %fusion.18 = f32[1024,512]{1,0:T(8,128)} fusion(bf16[1024,3072]{1,0:T(8,128)(2,1)} %all-gather.2.cloned.1.call-done, bf16[3072,512]{1,0:T(8,128)(2,1)} %param.8), kind=kOutput, calls=%fused_computation.27 | convolution fusion | flops 3221225472 | bytes 11534336 | tf_op jit(solution)/shard_map/dot_general | solution.py:19
  102.8 0.0 copy-done
  102.8 11.9 %convolution_convert_fusion = bf16[1024,3072]{1,0:T(8,128)(2,1)} fusion(bf16[512,3072]{1,0:T(8,128)(2,1)S(1)} %copy-done, f32[1024,512]{1,0:T(8,128)} %fusion.18, bf16[1024,3072]{1,0:T(8,128)(2,1)} %all-gather.2.cloned.1.call-done, bf16[3072,512]{1,0:T(8,128)(2,1)} %param.9), kind=kOutput, calls=%fused_computation | convolution fusion | flops 6448742400 | bytes 20971520 | tf_op jit(solution)/shard_map/dot_general | solution.py:22
  114.7 0.0 copy-start.1
  114.7 0.0 copy-start.2
  114.7 0.0 copy-start.3
  114.7 0.0 reduce-scatter.2.cloned.1.call-update
  114.7 0.6 copy-done.1
  115.4 0.0 copy-done.2
  115.4 0.0 copy-done.3
  115.4 0.1 convolution_bitcast_fusion
  115.5 83.4 %reduce-scatter.2.cloned.1.call-done = bf16[64,3072]{1,0:T(8,128)(2,1)} async-done(((bf16[1024,3072]{1,0:T(8,128)(2,1)}), bf16[64,3072]{1,0:T(8,128)(2,1)}) %reduce-scatter.2.cloned.1.call-update) | async-done | bytes 393232 | tf_op jit(solution)/shard_map/reduce_scatter | solution.py:25
  199.0 2.3 %convolution_convert_fusion.1 = bf16[128,3072]{1,0:T(8,128)(2,1)} fusion(bf16[64,3072]{1,0:T(8,128)(2,1)} %reduce-scatter.2.cloned.1.call-done, f32[64]{0:T(128)S(1)} %convolution_bitcast_fusion, s32[128]{0:T(128)S(1)} %copy-done.1), kind=kOutput, calls=%fused_computation.1 | convolution fusion | flops 51322880 | bytes 1180416 | tf_op jit(solution)/shard_map/cr,cd->rd/dot_general | solution.py:29
Async XLA Ops:
  6.5 96.2 %copy-start = (bf16[512,3072]{1,0:T(8,128)(2,1)S(1)}, bf16[512,3072]{1,0:T(8,128)(2,1)}, u32[]{:S(2)}) copy-start(bf16[512,3072]{1,0:T(8,128)(2,1)} %param.10) | copy-start | bytes 9437188
  6.5 87.8 %all-gather.2.cloned.1.call-start = ((), (), s32[]{:S(2)}) async-start(), calls=%async_computation.1 | async-start | bytes 6684672 | tf_op jit(solution)/shard_map/all_gather | solution.py:18
  8.9 190.1 %reduce-scatter.2.cloned.1.call-start = ((), (), s32[]{:S(2)}) async-start(), calls=%async_computation.2 | async-start | bytes 6684672 | tf_op jit(solution)/shard_map/reduce_scatter | solution.py:25
  114.7 0.7 copy-start.1
  114.7 0.7 copy-start.2
  114.7 0.7 copy-start.3
Sparse Core Ops, SparseCore 0:
  9.1 85.1 all-gather.1
  114.9 84.0 reduce-scatter.1
where the time goes:
time: 208 us
  waiting for transfers between devices  169 us (81%)
  matrix products  25.1 us (12%)
  between operations  13.4 us (6%)
    all_gather x1, waiting for transfers between devices, shards(): block = lax.all_gather(source, 'expert', axis=0, tiled=True)  85.4 us
    reduce_scatter x1, waiting for transfers between devices, shards(): lax.psum_scatter(terms.astype(jnp.bfloat16), 'expert', scatter_dimension=...  83.4 us
    dot_general x1, matrix products, shards(): jnp.dot(hidden, w_down, preferred_element_type=jnp.float32)  11.9 us
    dot_general x1, matrix products, shards(): gate = jnp.dot(block, w_gate, preferred_element_type=jnp.float32)  8.46 us
  transfers between devices with their start and end apart: 2, of which 2 were waited for; matrix products, arithmetic and copies ran while one was open for 0% of the time, Pallas kernels for 0%

commit v1 on v0

--- a/solution.py
+++ b/solution.py
@@ -15,7 +15,9 @@
     picker_half = picker.astype(jnp.bfloat16)
     source = jnp.dot(picker_half, tokens, preferred_element_type=jnp.float32).astype(jnp.bfloat16)
     row_share = jnp.dot(picker.astype(jnp.float32), share, precision=lax.Precision.HIGHEST)
-    block = lax.all_gather(source, "expert", axis=0, tiled=True)
+    block = jnp.concatenate(
+        lax.all_to_all(jnp.stack([source] * lax.axis_size("expert")), "expert", 0, 0), axis=0
+    )
     gate = jnp.dot(block, w_gate, preferred_element_type=jnp.float32)
     up = jnp.dot(block, w_up, preferred_element_type=jnp.float32)
     hidden = (jax.nn.silu(gate) * up).astype(jnp.bfloat16)

time: 208 us -> 272 us (1.31)
  blocking collectives: 0 us -> 149 us
  waiting for transfers between devices: 169 us -> 84.6 us
  matrix products: 25.1 us -> 20.6 us
  local copies, waits for them, and re-layouts: 0.67 us -> 4.1 us
    all_to_all x0 -> x1, blocking collectives: none -> 149 us  [shards(): lax.all_to_all(jnp.stack([source] * lax.axis_size('expert')), 'expert', 0...]
    all_gather x1 -> x0, waiting for transfers between devices: 85.4 us -> none  [shards(): block = lax.all_gather(source, 'expert', axis=0, tiled=True)]
    dot_general x1, matrix products: 8.46 us -> 4.76 us  [shards(): gate = jnp.dot(block, w_gate, preferred_element_type=jnp.float32)]
  transfers between devices with their start and end apart: 2 -> 1, of which waited for: 2 -> 1; matrix products, arithmetic and copies ran while one was open for 0% -> 0% of each run, Pallas kernels for 0% -> 0%
where the time goes in v1:
time: 272 us
  blocking collectives  149 us (55%)
  waiting for transfers between devices  84.6 us (31%)
  matrix products  20.6 us (8%)
  between operations  13.4 us (5%)
  local copies, waits for them, and re-layouts  4.1 us (2%)
    all_to_all x1, blocking collectives, shards(): lax.all_to_all(jnp.stack([source] * lax.axis_size('expert')), 'expert', 0...  149 us
    reduce_scatter x1, waiting for transfers between devices, shards(): lax.psum_scatter(terms.astype(jnp.bfloat16), 'expert', scatter_dimension=...  84.5 us
    dot_general x1, matrix products, shards(): jnp.dot(hidden, w_down, preferred_element_type=jnp.float32)  11.9 us
  transfers between devices with their start and end apart: 1, of which 1 were waited for; matrix products, arithmetic and copies ran while one was open for 0% of the time, Pallas kernels for 0%

profile of v1, /device:TPU:4, one launch (start us, length us, event | category | flops | bytes accessed | tf_op | source)
XLA Modules:
  0.0 271.7 jit_solution(11976089837104492171)
XLA Ops:
  6.5 0.0 copy-start
  6.5 0.0 reduce-scatter.2.cloned.1.call-start
  6.5 1.6 convolution_convert_fusion.2
  8.1 0.8 stack.2
  8.9 0.0 copy-start.3
  8.9 148.9 %all_to_all.5 = bf16[16,64,3072]{2,1,0:T(8,128)(2,1)S(1)} all-to-all(bf16[16,64,3072]{2,1,0:T(8,128)(2,1)S(1)} %stack.2), channel_id=1, replica_groups=mesh['dp'=16,'expert'=16] {'expert'}, dimensions={0} | all-to-all | bytes 12582912 | tf_op jit(solution)/shard_map/all_to_all | solution.py:19
  157.8 0.0 copy-start.1
  157.8 2.6 copy-done.1
  160.5 0.0 copy-done.3
  160.5 4.8 %fusion.18 = f32[1024,512]{1,0:T(8,128)} fusion(bf16[1024,3072]{1,0:T(8,128)(2,1)S(1)} %bitcast.22, bf16[3072,512]{1,0:T(8,128)(2,1)S(1)} %copy-done.3), kind=kOutput, calls=%fused_computation.27 | convolution fusion | flops 3221225472 | bytes 11534336 | tf_op jit(solution)/shard_map/dot_general | solution.py:21
  165.2 0.0 copy-done
  165.2 11.9 %convolution_convert_fusion = bf16[1024,3072]{1,0:T(8,128)(2,1)} fusion(bf16[512,3072]{1,0:T(8,128)(2,1)S(1)} %copy-done, f32[1024,512]{1,0:T(8,128)} %fusion.18, bf16[1024,3072]{1,0:T(8,128)(2,1)} %bitcast.23, bf16[3072,512]{1,0:T(8,128)(2,1)} %param.9), kind=kOutput, calls=%fused_computation | convolution fusion | flops 6448742400 | bytes 20971520 | tf_op jit(solution)/shard_map/dot_general | solution.py:24
  177.1 0.0 copy-start.2
  177.1 0.0 copy-start.4
  177.2 0.0 copy-start.5
  177.2 0.0 reduce-scatter.2.cloned.1.call-update
  177.2 0.6 copy-done.2
  177.8 0.0 copy-done.4
  177.8 0.0 copy-done.5
  177.8 0.1 convolution_bitcast_fusion
  178.0 84.5 %reduce-scatter.2.cloned.1.call-done = bf16[64,3072]{1,0:T(8,128)(2,1)} async-done(((bf16[1024,3072]{1,0:T(8,128)(2,1)}), bf16[64,3072]{1,0:T(8,128)(2,1)}) %reduce-scatter.2.cloned.1.call-update) | async-done | bytes 393232 | tf_op jit(solution)/shard_map/reduce_scatter | solution.py:27
  262.5 2.3 convolution_convert_fusion.1
Async XLA Ops:
  6.5 158.7 %copy-start = (bf16[512,3072]{1,0:T(8,128)(2,1)S(1)}, bf16[512,3072]{1,0:T(8,128)(2,1)}, u32[]{:S(2)}) copy-start(bf16[512,3072]{1,0:T(8,128)(2,1)} %param.10) | copy-start | bytes 9437188
  6.5 256.0 %reduce-scatter.2.cloned.1.call-start = ((), (), s32[]{:S(2)}) async-start(), calls=%async_computation.2 | async-start | bytes 6684672 | tf_op jit(solution)/shard_map/reduce_scatter | solution.py:27
  8.9 151.6 %copy-start.3 = (bf16[3072,512]{1,0:T(8,128)(2,1)S(1)}, bf16[3072,512]{1,0:T(8,128)(2,1)}, u32[]{:S(2)}) copy-start(bf16[3072,512]{1,0:T(8,128)(2,1)} %param.8) | copy-start | bytes 9437188
  157.8 2.6 copy-start.1
  177.1 0.7 copy-start.2
  177.1 0.7 copy-start.4
  177.2 0.7 copy-start.5
Sparse Core Ops, SparseCore 0:
  177.3 85.1 reduce-scatter.1
